TPU v7x, 256 devices: a whole 4x4x8 slice. The times are simulated.
256 devices in a mesh: panel: 8 (over z), rows: 32 (over y, x, core).
Axes of the slice: x: 4, y: 4, z: 8, core: 2. Of those that a mesh axis runs over, the one named last changes fastest.
Arguments:
- rhs_diag: bfloat16 [8, 8192, 128], P(None, 'rows'), may hold values from -6 to 6
- rhs_tall: bfloat16 [8, 16384, 128], P('panel', 'rows'), may hold values from -6 to 6
- diag_inverse: bfloat16 [8, 1024, 1024], P('panel'), may hold values from -0.1875 to 0.1875
- coupling: bfloat16 [8, 8192, 1024], P('panel', 'rows'), may hold values from -0.09375 to 0.09375
- tall_blocks: bfloat16 [8, 128, 128, 1024], P('panel', 'rows'), may hold values from -0.125 to 0.125
- sparsity: int32 [128, 8], P('rows', 'panel'), may hold values 0 or 1
Outputs:
- solution: float32 [8, 8, 1024, 128], P('panel', None, 'rows')
- tall_residual: float32 [8, 16384, 128], P('panel', 'rows')
All inputs are finite; a program needn't handle non-finite values. No bound on the sum of `sparsity` on one device may be relied on, other than what follows from the above.
Results may differ from a plain program's by a relative error of at most 0.0085.
Values may be sent and summed in bfloat16 or wider, within the bound.
No kernel may reach another device: no remote copies, remote signals or barrier semaphores. Data moves between devices by JAX's collectives and lax.ppermute only.
A program may use at most 64 MiB of HBM per device.

v0:
```python
import jax
import jax.numpy as jnp
from jax import lax
from jax.sharding import PartitionSpec as P


def shifted(block, axis, distance):
    devices = range(lax.axis_size(axis))
    route = [(i - distance, i) for i in devices if i - distance in devices]
    return lax.ppermute(block, axis, route)


def per_device(rhs_diag, rhs_tall, diag_inverse, coupling, tall_blocks, sparsity):
    panel_index = lax.axis_index("panel")
    rows_index = lax.axis_index("rows")
    panel_count = lax.axis_size("panel")
    rows_count = lax.axis_size("rows")
    batches, rows_here, columns = rhs_diag.shape
    panel_width = diag_inverse.shape[1]
    slice_rows = panel_width // rows_count
    blocks_here = tall_blocks.shape[1]
    block_rows = tall_blocks.shape[2]
    tall_rows = blocks_here * block_rows
    rows_panel = rows_index * rows_here // panel_width
    offset = jnp.clip(
        rows_index * rows_here - panel_index * panel_width, 0, panel_width - rows_here
    )
    inverse_cols = lax.dynamic_slice_in_dim(diag_inverse[0], offset, rows_here, 1)
    owner = rows_panel == panel_index
    is_later = rows_panel > panel_index
    coupling_here = coupling[0]
    tall_matrix = tall_blocks[0].reshape(tall_rows, panel_width)
    block_mask = jnp.repeat(sparsity[:, 0].astype(jnp.float32), block_rows)[:, None]

    def advance(tick_number, state_now):
        incoming, solutions, stored = state_now
        batch_now = tick_number - panel_index
        active = (batch_now >= 0) & (batch_now < batches)
        batch_safe = jnp.clip(batch_now, 0, batches - 1)
        rhs_now = lax.dynamic_index_in_dim(rhs_diag, batch_safe, 0, keepdims=False).astype(
            jnp.float32
        )
        reduced = (rhs_now - incoming).astype(jnp.bfloat16)
        partial_value = jnp.dot(inverse_cols, reduced, preferred_element_type=jnp.float32)
        partial_value = jnp.where(owner, partial_value, jnp.float32(0.0))
        summed_all = lax.psum(partial_value, "rows")
        own_rows = lax.dynamic_slice_in_dim(summed_all, rows_index * slice_rows, slice_rows, 0)
        solved = summed_all.astype(jnp.bfloat16)
        previous = lax.dynamic_index_in_dim(solutions, batch_safe, 0, keepdims=False)
        solutions = lax.dynamic_update_index_in_dim(
            solutions, jnp.where(active, own_rows, previous), batch_safe, 0
        )
        update = jnp.dot(coupling_here, solved, preferred_element_type=jnp.float32)
        outgoing = incoming + jnp.where(is_later, update, jnp.float32(0.0))
        earlier = lax.dynamic_index_in_dim(stored, batch_safe, 0, keepdims=False)
        stored = lax.dynamic_update_index_in_dim(
            stored, jnp.where(active, solved, earlier), batch_safe, 0
        )
        incoming = shifted(outgoing, "panel", 1)
        return (incoming, solutions, stored)

    stored = jnp.zeros((batches, panel_width, columns), jnp.bfloat16)
    initial = (
        jnp.zeros((rows_here, columns), jnp.float32),
        jnp.zeros((batches, slice_rows, columns), jnp.float32),
        stored,
    )
    tick_count = batches + panel_count - 1
    incoming, solutions, stored = lax.fori_loop(0, tick_count, advance, initial)
    tall_terms = (
        jnp.einsum("rw,bws->brs", tall_matrix, stored, preferred_element_type=jnp.float32)
        * block_mask
    )
    summed = lax.psum_scatter(tall_terms, "panel", scatter_dimension=0, tiled=True)
    tall_residual = rhs_tall.astype(jnp.float32) - summed
    return (solutions[None], tall_residual)


def solution(mesh):
    placed = (
        P(None, "rows", None),
        P("panel", "rows", None),
        P("panel", None, None),
        P("panel", "rows", None),
        P("panel", "rows", None, None),
        P("rows", "panel"),
    )
    return jax.shard_map(
        per_device,
        mesh=mesh,
        in_specs=placed,
        out_specs=(P("panel", None, "rows", None), P("panel", "rows", None)),
        check_vma=False,
    )
```

profile of v0, /device:TPU:2, one launch (start us, length us, event | category | flops | bytes accessed | tf_op | source)
XLA Modules:
  0.0 1989.9 jit_solution(4910491097746578890)
XLA Ops:
  12.2 1919.9 %while.19 = (s32[]{:T(128)}, f32[256,128]{0,1:T(8,128)S(1)}, f32[8,32,128]{2,1,0:T(8,128)}, bf16[8,1024,128]{1,2,0:T(8,128)(2,1)}, pred[]{:T(512)}, /*index=5*/p...) while((s32[]{:T(128)}, f32[256,128]{0,1:T(8,128)S(1)}, ...), condition=%wide.region_2.3_spmd, body=%wide.region_0.2_spmd.sunk | while | flops 135041024 | bytes 8307022 | solution.py:69
  16.7 115.6 %all-reduce.2.cloned.1.call-done = f32[1024,128]{0,1:T(8,128)} async-done(((f32[1024,128]{0,1:T(8,128)}), f32[1024,128]{0,1:T(8,128)}) %all-reduce.2.cloned.1.call-update) | async-done | bytes 524304 | tf_op jit(solution)/shard_map/while/body/eval_jaxpr/psum | solution.py:46
  134.3 3.5 collective-permute-start
  145.8 114.6 %all-reduce.2.cloned.1.call-done = f32[1024,128]{0,1:T(8,128)} async-done(((f32[1024,128]{0,1:T(8,128)}), f32[1024,128]{0,1:T(8,128)}) %all-reduce.2.cloned.1.call-update) | async-done | bytes 524304 | tf_op jit(solution)/shard_map/while/body/eval_jaxpr/psum | solution.py:46
  262.4 3.5 collective-permute-start
  273.9 114.6 %all-reduce.2.cloned.1.call-done = f32[1024,128]{0,1:T(8,128)} async-done(((f32[1024,128]{0,1:T(8,128)}), f32[1024,128]{0,1:T(8,128)}) %all-reduce.2.cloned.1.call-update) | async-done | bytes 524304 | tf_op jit(solution)/shard_map/while/body/eval_jaxpr/psum | solution.py:46
  390.5 3.5 collective-permute-start
  401.9 114.3 %all-reduce.2.cloned.1.call-done = f32[1024,128]{0,1:T(8,128)} async-done(((f32[1024,128]{0,1:T(8,128)}), f32[1024,128]{0,1:T(8,128)}) %all-reduce.2.cloned.1.call-update) | async-done | bytes 524304 | tf_op jit(solution)/shard_map/while/body/eval_jaxpr/psum | solution.py:46
  518.2 3.5 collective-permute-start
  529.7 114.3 %all-reduce.2.cloned.1.call-done = f32[1024,128]{0,1:T(8,128)} async-done(((f32[1024,128]{0,1:T(8,128)}), f32[1024,128]{0,1:T(8,128)}) %all-reduce.2.cloned.1.call-update) | async-done | bytes 524304 | tf_op jit(solution)/shard_map/while/body/eval_jaxpr/psum | solution.py:46
  646.0 3.5 collective-permute-start
  657.5 114.2 %all-reduce.2.cloned.1.call-done = f32[1024,128]{0,1:T(8,128)} async-done(((f32[1024,128]{0,1:T(8,128)}), f32[1024,128]{0,1:T(8,128)}) %all-reduce.2.cloned.1.call-update) | async-done | bytes 524304 | tf_op jit(solution)/shard_map/while/body/eval_jaxpr/psum | solution.py:46
  773.7 3.5 collective-permute-start
  785.2 114.6 %all-reduce.2.cloned.1.call-done = f32[1024,128]{0,1:T(8,128)} async-done(((f32[1024,128]{0,1:T(8,128)}), f32[1024,128]{0,1:T(8,128)}) %all-reduce.2.cloned.1.call-update) | async-done | bytes 524304 | tf_op jit(solution)/shard_map/while/body/eval_jaxpr/psum | solution.py:46
  901.8 3.5 collective-permute-start
  913.2 114.6 %all-reduce.2.cloned.1.call-done = f32[1024,128]{0,1:T(8,128)} async-done(((f32[1024,128]{0,1:T(8,128)}), f32[1024,128]{0,1:T(8,128)}) %all-reduce.2.cloned.1.call-update) | async-done | bytes 524304 | tf_op jit(solution)/shard_map/while/body/eval_jaxpr/psum | solution.py:46
  1029.8 3.5 collective-permute-start
  1041.3 114.6 %all-reduce.2.cloned.1.call-done = f32[1024,128]{0,1:T(8,128)} async-done(((f32[1024,128]{0,1:T(8,128)}), f32[1024,128]{0,1:T(8,128)}) %all-reduce.2.cloned.1.call-update) | async-done | bytes 524304 | tf_op jit(solution)/shard_map/while/body/eval_jaxpr/psum | solution.py:46
  1169.4 114.3 %all-reduce.2.cloned.1.call-done = f32[1024,128]{0,1:T(8,128)} async-done(((f32[1024,128]{0,1:T(8,128)}), f32[1024,128]{0,1:T(8,128)}) %all-reduce.2.cloned.1.call-update) | async-done | bytes 524304 | tf_op jit(solution)/shard_map/while/body/eval_jaxpr/psum | solution.py:46
  1285.7 3.5 collective-permute-start
  1297.1 114.6 %all-reduce.2.cloned.1.call-done = f32[1024,128]{0,1:T(8,128)} async-done(((f32[1024,128]{0,1:T(8,128)}), f32[1024,128]{0,1:T(8,128)}) %all-reduce.2.cloned.1.call-update) | async-done | bytes 524304 | tf_op jit(solution)/shard_map/while/body/eval_jaxpr/psum | solution.py:46
  1413.8 3.5 collective-permute-start
  1425.2 114.3 %all-reduce.2.cloned.1.call-done = f32[1024,128]{0,1:T(8,128)} async-done(((f32[1024,128]{0,1:T(8,128)}), f32[1024,128]{0,1:T(8,128)}) %all-reduce.2.cloned.1.call-update) | async-done | bytes 524304 | tf_op jit(solution)/shard_map/while/body/eval_jaxpr/psum | solution.py:46
  1541.6 3.5 collective-permute-start
  1553.0 114.6 %all-reduce.2.cloned.1.call-done = f32[1024,128]{0,1:T(8,128)} async-done(((f32[1024,128]{0,1:T(8,128)}), f32[1024,128]{0,1:T(8,128)}) %all-reduce.2.cloned.1.call-update) | async-done | bytes 524304 | tf_op jit(solution)/shard_map/while/body/eval_jaxpr/psum | solution.py:46
  1669.6 3.5 collective-permute-start
  1681.0 114.2 %all-reduce.2.cloned.1.call-done = f32[1024,128]{0,1:T(8,128)} async-done(((f32[1024,128]{0,1:T(8,128)}), f32[1024,128]{0,1:T(8,128)}) %all-reduce.2.cloned.1.call-update) | async-done | bytes 524304 | tf_op jit(solution)/shard_map/while/body/eval_jaxpr/psum | solution.py:46
  1797.3 3.5 collective-permute-start
  1808.8 114.3 %all-reduce.2.cloned.1.call-done = f32[1024,128]{0,1:T(8,128)} async-done(((f32[1024,128]{0,1:T(8,128)}), f32[1024,128]{0,1:T(8,128)}) %all-reduce.2.cloned.1.call-update) | async-done | bytes 524304 | tf_op jit(solution)/shard_map/while/body/eval_jaxpr/psum | solution.py:46
  1925.1 3.5 collective-permute-start
  1932.0 4.5 multiply_bitcast_fusion
  1937.5 43.4 %reduce-scatter.2.cloned.1.call-done = f32[1,512,128]{1,2,0:T(8,128)} async-done(((f32[8,512,128]{1,2,0:T(8,128)}), f32[1,512,128]{1,2,0:T(8,128)}) %reduce-scatter.2.cloned.1.call-update) | async-done | bytes 262160 | tf_op jit(solution)/shard_map/reduce_scatter | solution.py:74
  (258 shorter events, 160.2 us)
Async XLA Ops:
  12.2 120.1 %all-reduce.2.cloned.1.call-start = ((), (), s32[]{:S(2)}) async-start(), calls=%async_computation.2 | async-start | bytes 1048576 | tf_op jit(solution)/shard_map/while/body/eval_jaxpr/psum | solution.py:46
  134.3 6.9 collective-permute-start
  141.2 119.2 %all-reduce.2.cloned.1.call-start = ((), (), s32[]{:S(2)}) async-start(), calls=%async_computation.2 | async-start | bytes 1048576 | tf_op jit(solution)/shard_map/while/body/eval_jaxpr/psum | solution.py:46
  262.4 6.9 collective-permute-start
  269.3 119.1 %all-reduce.2.cloned.1.call-start = ((), (), s32[]{:S(2)}) async-start(), calls=%async_computation.2 | async-start | bytes 1048576 | tf_op jit(solution)/shard_map/while/body/eval_jaxpr/psum | solution.py:46
  390.5 6.9 collective-permute-start
  397.4 118.8 %all-reduce.2.cloned.1.call-start = ((), (), s32[]{:S(2)}) async-start(), calls=%async_computation.2 | async-start | bytes 1048576 | tf_op jit(solution)/shard_map/while/body/eval_jaxpr/psum | solution.py:46
  518.2 6.9 collective-permute-start
  525.1 118.8 %all-reduce.2.cloned.1.call-start = ((), (), s32[]{:S(2)}) async-start(), calls=%async_computation.2 | async-start | bytes 1048576 | tf_op jit(solution)/shard_map/while/body/eval_jaxpr/psum | solution.py:46
  644.0 7.3 copy-start.2
  646.0 6.9 collective-permute-start
  652.9 118.8 %all-reduce.2.cloned.1.call-start = ((), (), s32[]{:S(2)}) async-start(), calls=%async_computation.2 | async-start | bytes 1048576 | tf_op jit(solution)/shard_map/while/body/eval_jaxpr/psum | solution.py:46
  773.7 6.9 collective-permute-start
  780.6 119.1 %all-reduce.2.cloned.1.call-start = ((), (), s32[]{:S(2)}) async-start(), calls=%async_computation.2 | async-start | bytes 1048576 | tf_op jit(solution)/shard_map/while/body/eval_jaxpr/psum | solution.py:46
  901.8 6.9 collective-permute-start
  908.7 119.1 %all-reduce.2.cloned.1.call-start = ((), (), s32[]{:S(2)}) async-start(), calls=%async_computation.2 | async-start | bytes 1048576 | tf_op jit(solution)/shard_map/while/body/eval_jaxpr/psum | solution.py:46
  1029.8 6.9 collective-permute-start
  1036.7 119.1 %all-reduce.2.cloned.1.call-start = ((), (), s32[]{:S(2)}) async-start(), calls=%async_computation.2 | async-start | bytes 1048576 | tf_op jit(solution)/shard_map/while/body/eval_jaxpr/psum | solution.py:46
  1157.9 6.9 collective-permute-start
  1164.8 118.8 %all-reduce.2.cloned.1.call-start = ((), (), s32[]{:S(2)}) async-start(), calls=%async_computation.2 | async-start | bytes 1048576 | tf_op jit(solution)/shard_map/while/body/eval_jaxpr/psum | solution.py:46
  1285.7 6.9 collective-permute-start
  1292.6 119.1 %all-reduce.2.cloned.1.call-start = ((), (), s32[]{:S(2)}) async-start(), calls=%async_computation.2 | async-start | bytes 1048576 | tf_op jit(solution)/shard_map/while/body/eval_jaxpr/psum | solution.py:46
  1413.8 6.9 collective-permute-start
  1420.7 118.8 %all-reduce.2.cloned.1.call-start = ((), (), s32[]{:S(2)}) async-start(), calls=%async_computation.2 | async-start | bytes 1048576 | tf_op jit(solution)/shard_map/while/body/eval_jaxpr/psum | solution.py:46
  1541.6 6.9 collective-permute-start
  1548.5 119.1 %all-reduce.2.cloned.1.call-start = ((), (), s32[]{:S(2)}) async-start(), calls=%async_computation.2 | async-start | bytes 1048576 | tf_op jit(solution)/shard_map/while/body/eval_jaxpr/psum | solution.py:46
  1669.6 6.9 collective-permute-start
  1676.5 118.8 %all-reduce.2.cloned.1.call-start = ((), (), s32[]{:S(2)}) async-start(), calls=%async_computation.2 | async-start | bytes 1048576 | tf_op jit(solution)/shard_map/while/body/eval_jaxpr/psum | solution.py:46
  1797.3 6.9 collective-permute-start
  1804.2 118.8 %all-reduce.2.cloned.1.call-start = ((), (), s32[]{:S(2)}) async-start(), calls=%async_computation.2 | async-start | bytes 1048576 | tf_op jit(solution)/shard_map/while/body/eval_jaxpr/psum | solution.py:46
  1925.1 6.9 collective-permute-start
  1932.0 48.9 %reduce-scatter.2.cloned.1.call-start = ((), (), s32[]{:S(2)}) async-start(), calls=%async_computation.1 | async-start | bytes 2359296 | tf_op jit(solution)/shard_map/reduce_scatter | solution.py:74
  (17 other events, 109.2 us)
Sparse Core Ops, SparseCore 0:
  16.2 116.0 all-reduce.1
  145.2 115.0 all-reduce.1
  273.3 115.0 all-reduce.1
  401.1 115.0 all-reduce.1
  528.8 115.0 all-reduce.1
  656.6 115.0 all-reduce.1
  784.6 115.0 all-reduce.1
  912.7 115.0 all-reduce.1
  1040.8 115.0 all-reduce.1
  1168.5 115.0 all-reduce.1
  1296.6 115.0 all-reduce.1
  1424.4 115.0 all-reduce.1
  1552.5 115.0 all-reduce.1
  1680.2 115.0 all-reduce.1
  1807.9 115.0 all-reduce.1
Sparse Core Ops, SparseCore 1:
  1936.6 44.3 reduce-scatter.1
where the time goes:
time: 1990 us
  waiting for transfers between devices  1760 us (88%)
  local copies, waits for them, and re-layouts  66.1 us (3%)
  matrix products  51.9 us (3%)
  starting transfers between devices  51.8 us (3%)
  other arithmetic  42.9 us (2%)
    psum x15, waiting for transfers between devices, advance(): summed_all = lax.psum(partial_value, 'rows')  1720 us
    ppermute x15, starting transfers between devices, shifted(): return lax.ppermute(block, axis, route)  51.8 us
    reduce_scatter x1, waiting for transfers between devices, per_device(): lax.psum_scatter(tall_terms, 'panel', scatter_dimension=0, tiled=True)  43.4 us
  transfers between devices with their start and end apart: 31, of which 16 were waited for; matrix products, arithmetic and copies ran while one was open for 4% of the time, Pallas kernels for 0%

commit v1 on v0

--- a/solution.py
+++ b/solution.py
@@ -2,6 +2,7 @@
 import jax.numpy as jnp
 from jax import lax
 from jax.sharding import PartitionSpec as P
+from jax.lax import all_gather
 
 
 def shifted(block, axis, distance):
@@ -43,7 +44,7 @@
         reduced = (rhs_now - incoming).astype(jnp.bfloat16)
         partial_value = jnp.dot(inverse_cols, reduced, preferred_element_type=jnp.float32)
         partial_value = jnp.where(owner, partial_value, jnp.float32(0.0))
-        summed_all = lax.psum(partial_value, "rows")
+        summed_all = all_gather(partial_value, "rows").sum(axis=0)
         own_rows = lax.dynamic_slice_in_dim(summed_all, rows_index * slice_rows, slice_rows, 0)
         solved = summed_all.astype(jnp.bfloat16)
         previous = lax.dynamic_index_in_dim(solutions, batch_safe, 0, keepdims=False)

time: 1990 us -> 1830 us (0.920)
  waiting for transfers between devices: 1760 us -> 1250 us
  local copies, waits for them, and re-layouts: 66.1 us -> 307 us
  other arithmetic: 42.9 us -> 164 us
    psum x15 -> x0, waiting for transfers between devices: 1720 us -> none  [advance(): summed_all = lax.psum(partial_value, 'rows')]
    all_gather x0 -> x15, waiting for transfers between devices: none -> 1190 us  [advance(): summed_all = all_gather(partial_value, 'rows').sum(axis=0)]
    while x30 -> x15, local copies, waits for them, and re-layouts: 0.06 us -> 265 us
    reduce_sum x0 -> x15, other arithmetic: none -> 135 us  [advance(): summed_all = all_gather(partial_value, 'rows').sum(axis=0)]
  transfers between devices with their start and end apart: 31 -> 31, of which waited for: 16 -> 31; matrix products, arithmetic and copies ran while one was open for 4% -> 3% of each run, Pallas kernels for 0% -> 0%
where the time goes in v1:
time: 1830 us
  waiting for transfers between devices  1250 us (68%)
  local copies, waits for them, and re-layouts  307 us (17%)
  other arithmetic  164 us (9%)
  starting transfers between devices  52 us (3%)
  matrix products  41.4 us (2%)
    all_gather x15, waiting for transfers between devices, advance(): summed_all = all_gather(partial_value, 'rows').sum(axis=0)  1190 us
    while x15, local copies, waits for them, and re-layouts  265 us
    reduce_sum x15, other arithmetic, advance(): summed_all = all_gather(partial_value, 'rows').sum(axis=0)  135 us
    ppermute x15, starting transfers between devices, shifted(): return lax.ppermute(block, axis, route)  52 us
    reduce_scatter x1, waiting for transfers between devices, per_device(): lax.psum_scatter(tall_terms, 'panel', scatter_dimension=0, tiled=True)  43.2 us
  transfers between devices with their start and end apart: 31, of which 31 were waited for; matrix products, arithmetic and copies ran while one was open for 3% of the time, Pallas kernels for 0%

profile of v1, /device:TPU:2, one launch (start us, length us, event | category | flops | bytes accessed | tf_op | source)
XLA Modules:
  0.0 1828.6 jit_solution(2630523425063982597)
XLA Ops:
  12.1 1758.9 %while.19 = (s32[]{:T(128)}, f32[256,128]{0,1:T(8,128)S(1)}, f32[8,32,128]{2,1,0:T(8,128)}, bf16[8,1024,128]{1,2,0:T(8,128)(2,1)}, pred[]{:T(512)}, /*index=5*/p...) while((s32[]{:T(128)}, f32[256,128]{0,1:T(8,128)S(1)}, ...), condition=%wide.region_2.3_spmd, body=%wide.region_0.2_spmd.sunk | while | flops 138973184 | bytes 107331896 | solution.py:70
  15.1 81.0 %all-gather.5.cloned.1.call-done = f32[32768,128]{0,1:T(8,128)} async-done(((f32[1024,128]{0,1:T(8,128)}), f32[32768,128]{0,1:T(8,128)}) %all-gather.5.cloned.1.call-update) | async-done | bytes 16777232 | tf_op jit(solution)/shard_map/while/body/eval_jaxpr/all_gather | solution.py:47
  96.0 17.7 copy.26
  133.6 79.7 %all-gather.5.cloned.1.call-done = f32[32768,128]{0,1:T(8,128)} async-done(((f32[1024,128]{0,1:T(8,128)}), f32[32768,128]{0,1:T(8,128)}) %all-gather.5.cloned.1.call-update) | async-done | bytes 16777232 | tf_op jit(solution)/shard_map/while/body/eval_jaxpr/all_gather | solution.py:47
  213.4 17.7 copy.26
  250.9 79.7 %all-gather.5.cloned.1.call-done = f32[32768,128]{0,1:T(8,128)} async-done(((f32[1024,128]{0,1:T(8,128)}), f32[32768,128]{0,1:T(8,128)}) %all-gather.5.cloned.1.call-update) | async-done | bytes 16777232 | tf_op jit(solution)/shard_map/while/body/eval_jaxpr/all_gather | solution.py:47
  330.7 17.7 copy.26
  368.3 79.4 %all-gather.5.cloned.1.call-done = f32[32768,128]{0,1:T(8,128)} async-done(((f32[1024,128]{0,1:T(8,128)}), f32[32768,128]{0,1:T(8,128)}) %all-gather.5.cloned.1.call-update) | async-done | bytes 16777232 | tf_op jit(solution)/shard_map/while/body/eval_jaxpr/all_gather | solution.py:47
  447.7 17.7 copy.26
  485.3 79.4 %all-gather.5.cloned.1.call-done = f32[32768,128]{0,1:T(8,128)} async-done(((f32[1024,128]{0,1:T(8,128)}), f32[32768,128]{0,1:T(8,128)}) %all-gather.5.cloned.1.call-update) | async-done | bytes 16777232 | tf_op jit(solution)/shard_map/while/body/eval_jaxpr/all_gather | solution.py:47
  564.7 17.7 copy.26
  602.3 79.4 %all-gather.5.cloned.1.call-done = f32[32768,128]{0,1:T(8,128)} async-done(((f32[1024,128]{0,1:T(8,128)}), f32[32768,128]{0,1:T(8,128)}) %all-gather.5.cloned.1.call-update) | async-done | bytes 16777232 | tf_op jit(solution)/shard_map/while/body/eval_jaxpr/all_gather | solution.py:47
  681.7 17.7 copy.26
  719.3 79.7 %all-gather.5.cloned.1.call-done = f32[32768,128]{0,1:T(8,128)} async-done(((f32[1024,128]{0,1:T(8,128)}), f32[32768,128]{0,1:T(8,128)}) %all-gather.5.cloned.1.call-update) | async-done | bytes 16777232 | tf_op jit(solution)/shard_map/while/body/eval_jaxpr/all_gather | solution.py:47
  799.0 17.7 copy.26
  836.6 79.7 %all-gather.5.cloned.1.call-done = f32[32768,128]{0,1:T(8,128)} async-done(((f32[1024,128]{0,1:T(8,128)}), f32[32768,128]{0,1:T(8,128)}) %all-gather.5.cloned.1.call-update) | async-done | bytes 16777232 | tf_op jit(solution)/shard_map/while/body/eval_jaxpr/all_gather | solution.py:47
  916.4 17.7 copy.26
  954.0 79.7 %all-gather.5.cloned.1.call-done = f32[32768,128]{0,1:T(8,128)} async-done(((f32[1024,128]{0,1:T(8,128)}), f32[32768,128]{0,1:T(8,128)}) %all-gather.5.cloned.1.call-update) | async-done | bytes 16777232 | tf_op jit(solution)/shard_map/while/body/eval_jaxpr/all_gather | solution.py:47
  1033.7 17.7 copy.26
  1071.3 79.4 %all-gather.5.cloned.1.call-done = f32[32768,128]{0,1:T(8,128)} async-done(((f32[1024,128]{0,1:T(8,128)}), f32[32768,128]{0,1:T(8,128)}) %all-gather.5.cloned.1.call-update) | async-done | bytes 16777232 | tf_op jit(solution)/shard_map/while/body/eval_jaxpr/all_gather | solution.py:47
  1150.7 17.7 copy.26
  1188.3 79.7 %all-gather.5.cloned.1.call-done = f32[32768,128]{0,1:T(8,128)} async-done(((f32[1024,128]{0,1:T(8,128)}), f32[32768,128]{0,1:T(8,128)}) %all-gather.5.cloned.1.call-update) | async-done | bytes 16777232 | tf_op jit(solution)/shard_map/while/body/eval_jaxpr/all_gather | solution.py:47
  1268.0 17.7 copy.26
  1305.6 79.4 %all-gather.5.cloned.1.call-done = f32[32768,128]{0,1:T(8,128)} async-done(((f32[1024,128]{0,1:T(8,128)}), f32[32768,128]{0,1:T(8,128)}) %all-gather.5.cloned.1.call-update) | async-done | bytes 16777232 | tf_op jit(solution)/shard_map/while/body/eval_jaxpr/all_gather | solution.py:47
  1385.0 17.7 copy.26
  1422.6 79.7 %all-gather.5.cloned.1.call-done = f32[32768,128]{0,1:T(8,128)} async-done(((f32[1024,128]{0,1:T(8,128)}), f32[32768,128]{0,1:T(8,128)}) %all-gather.5.cloned.1.call-update) | async-done | bytes 16777232 | tf_op jit(solution)/shard_map/while/body/eval_jaxpr/all_gather | solution.py:47
  1502.3 17.7 copy.26
  1539.9 79.4 %all-gather.5.cloned.1.call-done = f32[32768,128]{0,1:T(8,128)} async-done(((f32[1024,128]{0,1:T(8,128)}), f32[32768,128]{0,1:T(8,128)}) %all-gather.5.cloned.1.call-update) | async-done | bytes 16777232 | tf_op jit(solution)/shard_map/while/body/eval_jaxpr/all_gather | solution.py:47
  1619.3 17.7 copy.26
  1656.9 79.4 %all-gather.5.cloned.1.call-done = f32[32768,128]{0,1:T(8,128)} async-done(((f32[1024,128]{0,1:T(8,128)}), f32[32768,128]{0,1:T(8,128)}) %all-gather.5.cloned.1.call-update) | async-done | bytes 16777232 | tf_op jit(solution)/shard_map/while/body/eval_jaxpr/all_gather | solution.py:47
  1736.4 17.7 copy.26
  1776.5 43.2 %reduce-scatter.2.cloned.1.call-done = f32[1,512,128]{1,2,0:T(8,128)} async-done(((f32[8,512,128]{1,2,0:T(8,128)}), f32[1,512,128]{1,2,0:T(8,128)}) %reduce-scatter.2.cloned.1.call-update) | async-done | bytes 262160 | tf_op jit(solution)/shard_map/reduce_scatter | solution.py:75
  (241 shorter events, 309.2 us)
Async XLA Ops:
  8.0 1.6 copy-start
  12.1 83.9 %all-gather.5.cloned.1.call-start = ((), (), s32[]{:S(2)}) async-start(), calls=%async_computation.2 | async-start | bytes 17301504 | tf_op jit(solution)/shard_map/while/body/eval_jaxpr/all_gather | solution.py:47
  124.1 6.6 collective-permute-start
  130.7 82.7 %all-gather.5.cloned.1.call-start = ((), (), s32[]{:S(2)}) async-start(), calls=%async_computation.2 | async-start | bytes 17301504 | tf_op jit(solution)/shard_map/while/body/eval_jaxpr/all_gather | solution.py:47
  241.4 6.6 collective-permute-start
  248.0 82.6 %all-gather.5.cloned.1.call-start = ((), (), s32[]{:S(2)}) async-start(), calls=%async_computation.2 | async-start | bytes 17301504 | tf_op jit(solution)/shard_map/while/body/eval_jaxpr/all_gather | solution.py:47
  358.7 6.6 collective-permute-start
  365.3 82.3 %all-gather.5.cloned.1.call-start = ((), (), s32[]{:S(2)}) async-start(), calls=%async_computation.2 | async-start | bytes 17301504 | tf_op jit(solution)/shard_map/while/body/eval_jaxpr/all_gather | solution.py:47
  475.7 6.6 collective-permute-start
  482.4 82.3 %all-gather.5.cloned.1.call-start = ((), (), s32[]{:S(2)}) async-start(), calls=%async_computation.2 | async-start | bytes 17301504 | tf_op jit(solution)/shard_map/while/body/eval_jaxpr/all_gather | solution.py:47
  592.7 6.6 collective-permute-start
  599.4 82.3 %all-gather.5.cloned.1.call-start = ((), (), s32[]{:S(2)}) async-start(), calls=%async_computation.2 | async-start | bytes 17301504 | tf_op jit(solution)/shard_map/while/body/eval_jaxpr/all_gather | solution.py:47
  709.7 6.6 collective-permute-start
  716.4 82.7 %all-gather.5.cloned.1.call-start = ((), (), s32[]{:S(2)}) async-start(), calls=%async_computation.2 | async-start | bytes 17301504 | tf_op jit(solution)/shard_map/while/body/eval_jaxpr/all_gather | solution.py:47
  827.1 6.6 collective-permute-start
  833.7 82.7 %all-gather.5.cloned.1.call-start = ((), (), s32[]{:S(2)}) async-start(), calls=%async_computation.2 | async-start | bytes 17301504 | tf_op jit(solution)/shard_map/while/body/eval_jaxpr/all_gather | solution.py:47
  944.4 6.6 collective-permute-start
  951.0 82.6 %all-gather.5.cloned.1.call-start = ((), (), s32[]{:S(2)}) async-start(), calls=%async_computation.2 | async-start | bytes 17301504 | tf_op jit(solution)/shard_map/while/body/eval_jaxpr/all_gather | solution.py:47
  1061.7 6.6 collective-permute-start
  1068.3 82.3 %all-gather.5.cloned.1.call-start = ((), (), s32[]{:S(2)}) async-start(), calls=%async_computation.2 | async-start | bytes 17301504 | tf_op jit(solution)/shard_map/while/body/eval_jaxpr/all_gather | solution.py:47
  1178.7 6.6 collective-permute-start
  1185.3 82.6 %all-gather.5.cloned.1.call-start = ((), (), s32[]{:S(2)}) async-start(), calls=%async_computation.2 | async-start | bytes 17301504 | tf_op jit(solution)/shard_map/while/body/eval_jaxpr/all_gather | solution.py:47
  1296.0 6.6 collective-permute-start
  1302.7 82.3 %all-gather.5.cloned.1.call-start = ((), (), s32[]{:S(2)}) async-start(), calls=%async_computation.2 | async-start | bytes 17301504 | tf_op jit(solution)/shard_map/while/body/eval_jaxpr/all_gather | solution.py:47
  1413.0 6.6 collective-permute-start
  1419.7 82.7 %all-gather.5.cloned.1.call-start = ((), (), s32[]{:S(2)}) async-start(), calls=%async_computation.2 | async-start | bytes 17301504 | tf_op jit(solution)/shard_map/while/body/eval_jaxpr/all_gather | solution.py:47
  1530.4 6.6 collective-permute-start
  1537.0 82.3 %all-gather.5.cloned.1.call-start = ((), (), s32[]{:S(2)}) async-start(), calls=%async_computation.2 | async-start | bytes 17301504 | tf_op jit(solution)/shard_map/while/body/eval_jaxpr/all_gather | solution.py:47
  1647.4 6.6 collective-permute-start
  1654.0 82.3 %all-gather.5.cloned.1.call-start = ((), (), s32[]{:S(2)}) async-start(), calls=%async_computation.2 | async-start | bytes 17301504 | tf_op jit(solution)/shard_map/while/body/eval_jaxpr/all_gather | solution.py:47
  1764.4 6.6 collective-permute-start
  1771.0 48.6 %reduce-scatter.2.cloned.1.call-start = ((), (), s32[]{:S(2)}) async-start(), calls=%async_computation.1 | async-start | bytes 2359296 | tf_op jit(solution)/shard_map/reduce_scatter | solution.py:75
  (1 other events, 0.9 us)
Sparse Core Ops, SparseCore 0:
  15.6 80.4 all-gather.4
  134.1 79.1 all-gather.4
  251.4 79.1 all-gather.4
  368.4 79.1 all-gather.4
  485.5 79.1 all-gather.4
  602.5 79.1 all-gather.4
  719.8 79.1 all-gather.4
  837.1 79.1 all-gather.4
  954.4 79.1 all-gather.4
  1071.4 79.1 all-gather.4
  1188.8 79.1 all-gather.4
  1305.8 79.1 all-gather.4
  1423.1 79.1 all-gather.4
  1540.1 79.1 all-gather.4
  1657.1 79.1 all-gather.4
Sparse Core Ops, SparseCore 1:
  1775.6 44.0 reduce-scatter.1
